TPU v7x, 128 devices: a whole 4x4x4 slice. The times are simulated.
128 devices in a mesh: dp: 16 (over x, y_hi, core), code: 8 (over y_lo, z).
Axes of the slice: x: 4, y: 4 (y_hi: 2, y_lo: 2; y = y_hi * 2 + y_lo), z: 4, core: 2. Of those that a mesh axis runs over, the one named last changes fastest.
Arguments:
- temporal_out: bfloat16 [2048, 4096], P('dp'), may hold values from -6 to 6
- depth_in: bfloat16 [8, 4096, 1024], P('code', 'dp'), may hold values from -0.09375 to 0.09375
- embed: bfloat16 [8, 1024, 1024], P('code'), may hold values from -6 to 6
- depth_w1: bfloat16 [8, 1024, 2112], P('code', None, 'dp'), may hold values from -0.1875 to 0.1875
- depth_w2: bfloat16 [8, 1024, 2112], P('code', None, 'dp'), may hold values from -0.125 to 0.125
- audio_tokens: int32 [2048, 8], P(None, 'code'), may hold values from 0 to 1023
- barge_mask: int32 [2048], P('dp'), may hold values 0 or 1
- out_grad: bfloat16 [2048, 8, 1024], P('dp', 'code'), may hold values from -6 to 6
Outputs:
- temporal_grad: bfloat16 [2048, 4096], P('dp', 'code')
- depth_in_grad: bfloat16 [8, 4096, 1024], P('code', 'dp')
- embed_grad: bfloat16 [8, 1024, 1024], P('code', 'dp')
- w1_grad: bfloat16 [8, 1024, 2112], P('code', None, 'dp')
- w2_grad: bfloat16 [8, 1024, 2112], P('code', None, 'dp')
All inputs are finite; a program needn't handle non-finite values. No bound on the sum of `barge_mask` on one device may be relied on, other than what follows from the above.
Results may differ from a plain program's by a relative error of at most 0.02.
Values may be sent and summed in bfloat16 or wider, within the bound.
No kernel may reach another device: no remote copies, remote signals or barrier semaphores. Data moves between devices by JAX's collectives and lax.ppermute only.
A program may use at most 128 MiB of HBM per device.

v0:
```python
import jax
import jax.numpy as jnp
from jax import lax
from jax.sharding import PartitionSpec as P

EPS = 1e-06


def shifted(block, axis, distance):
    devices = range(lax.axis_size(axis))
    route = [(i - distance, i) for i in devices if i - distance in devices]
    return lax.ppermute(block, axis, route)


def matmul(left, right):
    return jnp.dot(left, right, preferred_element_type=jnp.float32)


def contract_rows(left, right):
    return lax.dot_general(
        left, right, (((0,), (0,)), ((), ())), preferred_element_type=jnp.float32
    )


def contract_cols(left, right):
    return lax.dot_general(
        left, right, (((1,), (1,)), ((), ())), preferred_element_type=jnp.float32
    )


def silu_slope(values):
    sigma = jax.nn.sigmoid(values)
    return sigma * (1.0 + values * (1.0 - sigma))


def per_device(
    temporal_out, depth_in, embed, depth_w1, depth_w2, audio_tokens, barge_mask, out_grad
):
    dp_index = lax.axis_index("dp")
    n_code = lax.axis_size("code")
    own_rows = temporal_out.shape[0]
    projection = lax.all_gather(depth_in[0], "dp", axis=0, tiled=True)
    table = embed[0]
    token_all = audio_tokens[:, 0]
    token_own = lax.dynamic_slice_in_dim(token_all, dp_index * own_rows, own_rows, 0)
    depth_base = matmul(temporal_out, projection) + jnp.take(table, token_own, axis=0).astype(
        jnp.float32
    )
    width_depth = depth_base.shape[1]
    w_first, w_second = (
        lax.all_gather(depth_w1[0], "dp", axis=1, tiled=True),
        lax.all_gather(depth_w2[0], "dp", axis=1, tiled=True),
    )

    def depth_hidden(resid):
        scale = lax.rsqrt(jnp.mean(resid * resid, axis=-1, keepdims=True) + EPS)
        normed = (resid * scale).astype(jnp.bfloat16)
        pre_act = matmul(normed, w_first)
        active = jax.nn.silu(pre_act).astype(jnp.bfloat16)
        return (scale, normed, pre_act, active)

    def forward_turn(turn_index, incoming):
        resid = depth_base + incoming.astype(jnp.float32)
        scale, normed, pre_act, active = depth_hidden(resid)
        state = (resid + contract_cols(active, w_second)).astype(jnp.bfloat16)
        return shifted(state, "code", 1)

    start_state = jnp.zeros((own_rows, width_depth), jnp.bfloat16)
    incoming = lax.fori_loop(0, n_code - 1, forward_turn, start_state)
    resid = depth_base + incoming.astype(jnp.float32)
    scale, normed, pre_act, active = depth_hidden(resid)
    unit_rows = resid * scale
    derivative = silu_slope(pre_act)
    cotangent = out_grad[:, 0, :].astype(jnp.float32) * barge_mask.astype(jnp.float32)[:, None]

    def depth_back(from_next):
        state_slope = cotangent + from_next.astype(jnp.float32)
        slope_b = state_slope.astype(jnp.bfloat16)
        pre_slope = (matmul(slope_b, w_second) * derivative).astype(jnp.bfloat16)
        norm_slope = contract_cols(pre_slope, w_first)
        carried = (
            state_slope
            + scale
            * (norm_slope - unit_rows * jnp.mean(norm_slope * unit_rows, axis=-1, keepdims=True))
        ).astype(jnp.bfloat16)
        return (carried, slope_b, pre_slope)

    def backward_turn(turn_index, from_next):
        return shifted(depth_back(from_next)[0], "code", -1)

    from_next = lax.fori_loop(0, n_code - 1, backward_turn, start_state)
    carried, slope_b, pre_slope = depth_back(from_next)
    first_grad, second_grad = (
        lax.psum_scatter(
            contract_rows(normed, pre_slope).astype(jnp.bfloat16),
            "dp",
            scatter_dimension=1,
            tiled=True,
        ).astype(jnp.float32),
        lax.psum_scatter(
            contract_rows(slope_b, active).astype(jnp.bfloat16),
            "dp",
            scatter_dimension=1,
            tiled=True,
        ).astype(jnp.float32),
    )
    temporal_grad = lax.psum_scatter(
        contract_cols(carried, projection).astype(jnp.bfloat16),
        "code",
        scatter_dimension=1,
        tiled=True,
    )
    vocab_ids = lax.broadcasted_iota(jnp.int32, (1, table.shape[0]), 1)
    onehot = (token_own[:, None] == vocab_ids).astype(jnp.bfloat16)
    proj_grad, table_grad = (
        lax.psum_scatter(
            contract_rows(temporal_out, carried).astype(jnp.bfloat16),
            "dp",
            scatter_dimension=0,
            tiled=True,
        ).astype(jnp.float32),
        lax.psum_scatter(
            contract_rows(onehot, carried).astype(jnp.bfloat16),
            "dp",
            scatter_dimension=0,
            tiled=True,
        ).astype(jnp.float32),
    )
    return (
        temporal_grad,
        proj_grad.astype(jnp.bfloat16)[None],
        table_grad.astype(jnp.bfloat16)[None],
        first_grad.astype(jnp.bfloat16)[None],
        second_grad.astype(jnp.bfloat16)[None],
    )


def solution(mesh):
    in_specs = (
        P("dp", None),
        P("code", "dp", None),
        P("code", None, None),
        P("code", None, "dp"),
        P("code", None, "dp"),
        P(None, "code"),
        P("dp"),
        P("dp", "code", None),
    )
    out_specs = (
        P("dp", "code"),
        P("code", "dp", None),
        P("code", "dp", None),
        P("code", None, "dp"),
        P("code", None, "dp"),
    )
    return jax.shard_map(
        per_device, mesh=mesh, in_specs=in_specs, out_specs=out_specs, check_vma=False
    )
```

profile of v0, /device:TPU:0, one launch (start us, length us, event | category | flops | bytes accessed | tf_op | source)
XLA Modules:
  0.0 786.8 jit_solution(18314862474826231828)
XLA Ops:
  7.2 2.4 copy.25
  9.7 2.2 copy.26
  15.0 71.7 %all-gather.9.cloned.1.call-done = bf16[1,1024,2112]{1,0,2:T(2,128)(2,1)} async-done(((bf16[1,1024,132]{1,0,2:T(2,128)(2,1)}), bf16[1,1024,2112]{1,0,2:T(2,128)(2,1)}) %all-gather.9.cloned.1.call-update) | async-done | bytes 4325392 | tf_op jit(solution)/shard_map/all_gather | solution.py:51
  86.7 20.8 %copy.34 = bf16[1,1024,2112]{2,1,0:T(8,128)(2,1)} copy(bf16[1,1024,2112]{1,0,2:T(2,128)(2,1)} %all-gather.9.cloned.1.call-done) | data formatting | bytes 8650752
  107.5 53.2 %all-gather.11.cloned.1.call-done = bf16[1,1024,2112]{1,0,2:T(2,128)(2,1)} async-done(((bf16[1,1024,132]{1,0,2:T(2,128)(2,1)}), bf16[1,1024,2112]{1,0,2:T(2,128)(2,1)}) %all-gather.11.cloned.1.call-update) | async-done | bytes 4325392 | tf_op jit(solution)/shard_map/all_gather | solution.py:52
  160.8 20.9 %copy.35 = bf16[1,1024,2112]{2,1,0:T(8,128)(2,1)} copy(bf16[1,1024,2112]{1,0,2:T(2,128)(2,1)} %all-gather.11.cloned.1.call-done) | data formatting | bytes 8650752
  181.7 52.1 %all-gather.7.cloned.1.call-done = bf16[1,4096,1024]{2,1,0:T(8,128)(2,1)} async-done(((bf16[1,256,1024]{2,1,0:T(8,128)(2,1)}), bf16[1,4096,1024]{2,1,0:T(8,128)(2,1)}) %all-gather.7.cloned.1.call-update) | async-done | bytes 8388624 | tf_op jit(solution)/shard_map/all_gather | solution.py:42
  233.7 4.6 fusion.35
  238.4 120.9 %while.20 = (s32[]{:T(128)}, bf16[128,1024]{1,0:T(8,128)(2,1)S(1)}, f32[128,1024]{1,0:T(8,128)S(1)}, bf16[1024,2112]{1,0:T(8,128)(2,1)}, bf16[1024,2112]{1,0:T(8,128)(2,1)}, /*index=5*/s32[]{:T(128)}) while((s32[]{:T(128)}, bf16[128,1024]{1,0:T(8,128)(2,1)S(1)}, f32[128,1024]{1,0:T(8,128)S(1)}, bf16[1024,2112]{1,0:T(8,128)(2,1)}, ...), condition=%wide.region_2.3_spmd, body=%wide.region_0.0_spmd.sunk | while | flops 1110220928 | bytes 11536493 | solution.py:69
  238.6 8.2 %fusion.71 = bf16[128,1024]{1,0:T(8,128)(2,1)S(1)} fusion(bf16[1024,2112]{1,0:T(8,128)(2,1)} %get-tuple-element.265, bf16[1024,2112]{1,0:T(8,128)(2,1)} %get-tuple-element.264, f32[128,1024]{1,0:T(8,128)S(1)} %get-tuple-element.263, bf16[128,1024]{1,0:T(8,128)(2,1)S(1)} %get-tuple-element.256, f32[128]{0:T(128)S(1)} %add_rsqrt_fusion.3), kind=kOutput, calls=%fused_computation.2.clone.1 | convolution fusion | flops 1109696512 | bytes 9699840 | tf_op jit(solution)/shard_map/while/body/eval_jaxpr/dot_general | solution.py:26
  246.8 3.5 collective-permute-start
  250.2 5.9 collective-permute-done
  256.3 8.2 %fusion.71 = bf16[128,1024]{1,0:T(8,128)(2,1)S(1)} fusion(bf16[1024,2112]{1,0:T(8,128)(2,1)} %get-tuple-element.265, bf16[1024,2112]{1,0:T(8,128)(2,1)} %get-tuple-element.264, f32[128,1024]{1,0:T(8,128)S(1)} %get-tuple-element.263, bf16[128,1024]{1,0:T(8,128)(2,1)S(1)} %get-tuple-element.256, f32[128]{0:T(128)S(1)} %add_rsqrt_fusion.3), kind=kOutput, calls=%fused_computation.2.clone.1 | convolution fusion | flops 1109696512 | bytes 9699840 | tf_op jit(solution)/shard_map/while/body/eval_jaxpr/dot_general | solution.py:26
  264.5 4.4 collective-permute-start
  268.9 5.1 collective-permute-done
  274.2 8.2 %fusion.71 = bf16[128,1024]{1,0:T(8,128)(2,1)S(1)} fusion(bf16[1024,2112]{1,0:T(8,128)(2,1)} %get-tuple-element.265, bf16[1024,2112]{1,0:T(8,128)(2,1)} %get-tuple-element.264, f32[128,1024]{1,0:T(8,128)S(1)} %get-tuple-element.263, bf16[128,1024]{1,0:T(8,128)(2,1)S(1)} %get-tuple-element.256, f32[128]{0:T(128)S(1)} %add_rsqrt_fusion.3), kind=kOutput, calls=%fused_computation.2.clone.1 | convolution fusion | flops 1109696512 | bytes 9699840 | tf_op jit(solution)/shard_map/while/body/eval_jaxpr/dot_general | solution.py:26
  282.4 4.4 collective-permute-start
  286.8 4.2 collective-permute-done
  291.1 8.2 %fusion.71 = bf16[128,1024]{1,0:T(8,128)(2,1)S(1)} fusion(bf16[1024,2112]{1,0:T(8,128)(2,1)} %get-tuple-element.265, bf16[1024,2112]{1,0:T(8,128)(2,1)} %get-tuple-element.264, f32[128,1024]{1,0:T(8,128)S(1)} %get-tuple-element.263, bf16[128,1024]{1,0:T(8,128)(2,1)S(1)} %get-tuple-element.256, f32[128]{0:T(128)S(1)} %add_rsqrt_fusion.3), kind=kOutput, calls=%fused_computation.2.clone.1 | convolution fusion | flops 1109696512 | bytes 9699840 | tf_op jit(solution)/shard_map/while/body/eval_jaxpr/dot_general | solution.py:26
  299.3 4.4 collective-permute-start
  303.7 3.9 collective-permute-done
  307.7 8.2 %fusion.71 = bf16[128,1024]{1,0:T(8,128)(2,1)S(1)} fusion(bf16[1024,2112]{1,0:T(8,128)(2,1)} %get-tuple-element.265, bf16[1024,2112]{1,0:T(8,128)(2,1)} %get-tuple-element.264, f32[128,1024]{1,0:T(8,128)S(1)} %get-tuple-element.263, bf16[128,1024]{1,0:T(8,128)(2,1)S(1)} %get-tuple-element.256, f32[128]{0:T(128)S(1)} %add_rsqrt_fusion.3), kind=kOutput, calls=%fused_computation.2.clone.1 | convolution fusion | flops 1109696512 | bytes 9699840 | tf_op jit(solution)/shard_map/while/body/eval_jaxpr/dot_general | solution.py:26
  315.9 4.4 collective-permute-start
  320.3 3.9 collective-permute-done
  324.3 8.2 %fusion.71 = bf16[128,1024]{1,0:T(8,128)(2,1)S(1)} fusion(bf16[1024,2112]{1,0:T(8,128)(2,1)} %get-tuple-element.265, bf16[1024,2112]{1,0:T(8,128)(2,1)} %get-tuple-element.264, f32[128,1024]{1,0:T(8,128)S(1)} %get-tuple-element.263, bf16[128,1024]{1,0:T(8,128)(2,1)S(1)} %get-tuple-element.256, f32[128]{0:T(128)S(1)} %add_rsqrt_fusion.3), kind=kOutput, calls=%fused_computation.2.clone.1 | convolution fusion | flops 1109696512 | bytes 9699840 | tf_op jit(solution)/shard_map/while/body/eval_jaxpr/dot_general | solution.py:26
  332.5 4.4 collective-permute-start
  336.9 3.9 collective-permute-done
  340.9 8.2 %fusion.71 = bf16[128,1024]{1,0:T(8,128)(2,1)S(1)} fusion(bf16[1024,2112]{1,0:T(8,128)(2,1)} %get-tuple-element.265, bf16[1024,2112]{1,0:T(8,128)(2,1)} %get-tuple-element.264, f32[128,1024]{1,0:T(8,128)S(1)} %get-tuple-element.263, bf16[128,1024]{1,0:T(8,128)(2,1)S(1)} %get-tuple-element.256, f32[128]{0:T(128)S(1)} %add_rsqrt_fusion.3), kind=kOutput, calls=%fused_computation.2.clone.1 | convolution fusion | flops 1109696512 | bytes 9699840 | tf_op jit(solution)/shard_map/while/body/eval_jaxpr/dot_general | solution.py:26
  349.1 6.4 collective-permute-start
  355.5 3.9 collective-permute-done
  359.6 6.1 add_multiply_fusion
  365.7 133.4 %while.21 = (s32[]{:T(128)}, bf16[128,1024]{1,0:T(8,128)(2,1)S(1)}, f32[128,1024]{1,0:T(8,128)S(1)}, f32[128,1]{0,1:T(1,128)S(1)}, bf16[1024,2112]{1,0:T(8,128)(...) while((s32[]{:T(128)}, bf16[128,1024]{1,0:T(8,128)(2,1)S(1)}, ...), condition=%wide.region_6.7_spmd, body=%wide.region_4.6_spmd.sunk | while | flops 1109409792 | bytes 14715525 | solution.py:91
  365.7 8.2 %multiply_reduce_fusion.7 = (f32[128]{0:T(128)S(1)}, f32[128,1024]{1,0:T(8,128)S(1)}) fusion(f32[128,1024]{1,0:T(8,128)S(1)} %get-tuple-element.292, bf16[1024,2112]{1,0:T(8,128)(2,1)} %get-tuple-element.291, f32[128,2112]{0,1:T(8,128)S(1)} %get-tuple-element.290, bf16[1024,2112]{1,0:T(8,128)(2,1)} %get-tuple-element.289, ...), kind=kOutput, calls=%fused_computation.16.clone.1 | convolution fusion | flops 1108492160 | bytes 11567616 | tf_op jit(solution)/shard_map/while/body/eval_jaxpr/dot_general | solution.py:26
  374.2 1.3 collective-permute-start.1
  375.5 9.5 %collective-permute-done.1 = bf16[128,1024]{1,0:T(8,128)(2,1)S(1)} collective-permute-done((bf16[128,1024]{1,0:T(8,128)(2,1)S(1)}, bf16[128,1024]{1,0:T(8,128)(2,1)S(1)}, u32[]{:S(2)}, u32[]{:S(2)}) %collective-permute-start.1) | collective-permute-done | bytes 262176 | tf_op jit(solution)/shard_map/while/body/eval_jaxpr/ppermute | solution.py:12
  385.0 8.2 %multiply_reduce_fusion.7 = (f32[128]{0:T(128)S(1)}, f32[128,1024]{1,0:T(8,128)S(1)}) fusion(f32[128,1024]{1,0:T(8,128)S(1)} %get-tuple-element.292, bf16[1024,2112]{1,0:T(8,128)(2,1)} %get-tuple-element.291, f32[128,2112]{0,1:T(8,128)S(1)} %get-tuple-element.290, bf16[1024,2112]{1,0:T(8,128)(2,1)} %get-tuple-element.289, ...), kind=kOutput, calls=%fused_computation.16.clone.1 | convolution fusion | flops 1108492160 | bytes 11567616 | tf_op jit(solution)/shard_map/while/body/eval_jaxpr/dot_general | solution.py:26
  393.4 1.3 collective-permute-start.1
  394.7 9.5 %collective-permute-done.1 = bf16[128,1024]{1,0:T(8,128)(2,1)S(1)} collective-permute-done((bf16[128,1024]{1,0:T(8,128)(2,1)S(1)}, bf16[128,1024]{1,0:T(8,128)(2,1)S(1)}, u32[]{:S(2)}, u32[]{:S(2)}) %collective-permute-start.1) | collective-permute-done | bytes 262176 | tf_op jit(solution)/shard_map/while/body/eval_jaxpr/ppermute | solution.py:12
  404.3 8.2 %multiply_reduce_fusion.7 = (f32[128]{0:T(128)S(1)}, f32[128,1024]{1,0:T(8,128)S(1)}) fusion(f32[128,1024]{1,0:T(8,128)S(1)} %get-tuple-element.292, bf16[1024,2112]{1,0:T(8,128)(2,1)} %get-tuple-element.291, f32[128,2112]{0,1:T(8,128)S(1)} %get-tuple-element.290, bf16[1024,2112]{1,0:T(8,128)(2,1)} %get-tuple-element.289, ...), kind=kOutput, calls=%fused_computation.16.clone.1 | convolution fusion | flops 1108492160 | bytes 11567616 | tf_op jit(solution)/shard_map/while/body/eval_jaxpr/dot_general | solution.py:26
  412.7 1.3 collective-permute-start.1
  414.0 9.5 %collective-permute-done.1 = bf16[128,1024]{1,0:T(8,128)(2,1)S(1)} collective-permute-done((bf16[128,1024]{1,0:T(8,128)(2,1)S(1)}, bf16[128,1024]{1,0:T(8,128)(2,1)S(1)}, u32[]{:S(2)}, u32[]{:S(2)}) %collective-permute-start.1) | collective-permute-done | bytes 262176 | tf_op jit(solution)/shard_map/while/body/eval_jaxpr/ppermute | solution.py:12
  423.5 8.2 %multiply_reduce_fusion.7 = (f32[128]{0:T(128)S(1)}, f32[128,1024]{1,0:T(8,128)S(1)}) fusion(f32[128,1024]{1,0:T(8,128)S(1)} %get-tuple-element.292, bf16[1024,2112]{1,0:T(8,128)(2,1)} %get-tuple-element.291, f32[128,2112]{0,1:T(8,128)S(1)} %get-tuple-element.290, bf16[1024,2112]{1,0:T(8,128)(2,1)} %get-tuple-element.289, ...), kind=kOutput, calls=%fused_computation.16.clone.1 | convolution fusion | flops 1108492160 | bytes 11567616 | tf_op jit(solution)/shard_map/while/body/eval_jaxpr/dot_general | solution.py:26
  431.9 1.3 collective-permute-start.1
  433.2 9.5 %collective-permute-done.1 = bf16[128,1024]{1,0:T(8,128)(2,1)S(1)} collective-permute-done((bf16[128,1024]{1,0:T(8,128)(2,1)S(1)}, bf16[128,1024]{1,0:T(8,128)(2,1)S(1)}, u32[]{:S(2)}, u32[]{:S(2)}) %collective-permute-start.1) | collective-permute-done | bytes 262176 | tf_op jit(solution)/shard_map/while/body/eval_jaxpr/ppermute | solution.py:12
  442.8 8.2 %multiply_reduce_fusion.7 = (f32[128]{0:T(128)S(1)}, f32[128,1024]{1,0:T(8,128)S(1)}) fusion(f32[128,1024]{1,0:T(8,128)S(1)} %get-tuple-element.292, bf16[1024,2112]{1,0:T(8,128)(2,1)} %get-tuple-element.291, f32[128,2112]{0,1:T(8,128)S(1)} %get-tuple-element.290, bf16[1024,2112]{1,0:T(8,128)(2,1)} %get-tuple-element.289, ...), kind=kOutput, calls=%fused_computation.16.clone.1 | convolution fusion | flops 1108492160 | bytes 11567616 | tf_op jit(solution)/shard_map/while/body/eval_jaxpr/dot_general | solution.py:26
  451.2 1.3 collective-permute-start.1
  452.5 9.1 %collective-permute-done.1 = bf16[128,1024]{1,0:T(8,128)(2,1)S(1)} collective-permute-done((bf16[128,1024]{1,0:T(8,128)(2,1)S(1)}, bf16[128,1024]{1,0:T(8,128)(2,1)S(1)}, u32[]{:S(2)}, u32[]{:S(2)}) %collective-permute-start.1) | collective-permute-done | bytes 262176 | tf_op jit(solution)/shard_map/while/body/eval_jaxpr/ppermute | solution.py:12
  461.6 8.2 %multiply_reduce_fusion.7 = (f32[128]{0:T(128)S(1)}, f32[128,1024]{1,0:T(8,128)S(1)}) fusion(f32[128,1024]{1,0:T(8,128)S(1)} %get-tuple-element.292, bf16[1024,2112]{1,0:T(8,128)(2,1)} %get-tuple-element.291, f32[128,2112]{0,1:T(8,128)S(1)} %get-tuple-element.290, bf16[1024,2112]{1,0:T(8,128)(2,1)} %get-tuple-element.289, ...), kind=kOutput, calls=%fused_computation.16.clone.1 | convolution fusion | flops 1108492160 | bytes 11567616 | tf_op jit(solution)/shard_map/while/body/eval_jaxpr/dot_general | solution.py:26
  471.3 9.1 %collective-permute-done.1 = bf16[128,1024]{1,0:T(8,128)(2,1)S(1)} collective-permute-done((bf16[128,1024]{1,0:T(8,128)(2,1)S(1)}, bf16[128,1024]{1,0:T(8,128)(2,1)S(1)}, u32[]{:S(2)}, u32[]{:S(2)}) %collective-permute-start.1) | collective-permute-done | bytes 262176 | tf_op jit(solution)/shard_map/while/body/eval_jaxpr/ppermute | solution.py:12
  480.4 8.2 %multiply_reduce_fusion.7 = (f32[128]{0:T(128)S(1)}, f32[128,1024]{1,0:T(8,128)S(1)}) fusion(f32[128,1024]{1,0:T(8,128)S(1)} %get-tuple-element.292, bf16[1024,2112]{1,0:T(8,128)(2,1)} %get-tuple-element.291, f32[128,2112]{0,1:T(8,128)S(1)} %get-tuple-element.290, bf16[1024,2112]{1,0:T(8,128)(2,1)} %get-tuple-element.289, ...), kind=kOutput, calls=%fused_computation.16.clone.1 | convolution fusion | flops 1108492160 | bytes 11567616 | tf_op jit(solution)/shard_map/while/body/eval_jaxpr/dot_general | solution.py:26
  490.1 9.1 %collective-permute-done.1 = bf16[128,1024]{1,0:T(8,128)(2,1)S(1)} collective-permute-done((bf16[128,1024]{1,0:T(8,128)(2,1)S(1)}, bf16[128,1024]{1,0:T(8,128)(2,1)S(1)}, u32[]{:S(2)}, u32[]{:S(2)}) %collective-permute-start.1) | collective-permute-done | bytes 262176 | tf_op jit(solution)/shard_map/while/body/eval_jaxpr/ppermute | solution.py:12
  499.2 5.4 fusion.30
  504.6 5.3 multiply_reduce_fusion.2
  510.2 5.6 convert_bitcast_fusion
  515.9 7.2 fusion.17
  523.8 2.2 convolution_convert_fusion.2
  526.0 3.3 convolution_convert_fusion.1
  529.3 3.4 convolution_convert_fusion
  532.8 118.3 %fusion.49 = (bf16[1024,136]{0,1:T(8,128)(2,1)S(1)}, bf16[1024,136]{0,1:T(8,128)(2,1)S(1)}) fusion(bf16[1024,2112]{0,1:T(8,128)(2,1)} %convolution_convert_fusion.1, bf16[1024,2112]{0,1:T(8,128)(2,1)} %convolution_convert_fusion), kind=kCustom, calls=%all-reduce-scatter.2 | all-reduce-scatter fusion | flops 4456449 | bytes 9208320
  651.1 10.0 %collective-permute-start.3 = (bf16[1024,60]{0,1:T(8,128)(2,1)S(1)}, bf16[1024,60]{0,1:T(8,128)(2,1)S(1)}, u32[]{:S(2)}, u32[]{:S(2)}) collective-permute-start(bf16[1024,60]{0,1:T(8,128)(2,1)S(1)} %slice.3), channel_id=1, source_target_pairs={{0,8},{8,16},{16,24},{24,32},{32,40},{40,48},{48,56},{56,64},{64,7... | collective-permute-start | bytes 368648
  661.1 6.5 collective-permute-start.2
  672.1 2.0 copy.31
  674.2 31.9 %reduce-scatter.8.cloned.1.call-done = bf16[128,512]{1,0:T(8,128)(2,1)} async-done(((bf16[128,4096]{1,0:T(8,128)(2,1)}), bf16[128,512]{1,0:T(8,128)(2,1)}) %reduce-scatter.8.cloned.1.call-update) | async-done | bytes 131088 | tf_op jit(solution)/shard_map/reduce_scatter | solution.py:107
  706.1 73.9 %reduce-scatter.12.cloned.1.call-done = bf16[64,1024]{1,0:T(8,128)(2,1)} async-done(((bf16[1024,1024]{1,0:T(8,128)(2,1)}), bf16[64,1024]{1,0:T(8,128)(2,1)}) %reduce-scatter.12.cloned.1.call-update) | async-done | bytes 131088 | tf_op jit(solution)/shard_map/reduce_scatter | solution.py:122
  (81 shorter events, 13.4 us)
Async XLA Ops:
  7.2 6.8 copy-start
  7.2 7.7 copy-start.4
  7.2 79.5 %all-gather.9.cloned.1.call-start = ((), (), s32[]{:S(2)}) async-start(), calls=%async_computation.7 | async-start | bytes 9191424 | tf_op jit(solution)/shard_map/all_gather | solution.py:51
  9.6 151.1 %all-gather.11.cloned.1.call-start = ((), (), s32[]{:S(2)}) async-start(), calls=%async_computation.8 | async-start | bytes 9191424 | tf_op jit(solution)/shard_map/all_gather | solution.py:52
  11.9 221.9 %all-gather.7.cloned.1.call-start = ((), (), s32[]{:S(2)}) async-start(), calls=%async_computation.6 | async-start | bytes 8912896 | tf_op jit(solution)/shard_map/all_gather | solution.py:42
  12.6 659.5 %reduce-scatter.10.cloned.1.call-start = ((), (), s32[]{:S(2)}) async-start(), calls=%async_computation.4 | async-start | bytes 8912896 | tf_op jit(solution)/shard_map/reduce_scatter | solution.py:116
  107.5 126.2 %copy-start.2 = (bf16[128,4096]{1,0:T(8,128)(2,1)S(1)}, bf16[128,4096]{1,0:T(8,128)(2,1)}, u32[]{:S(2)}) copy-start(bf16[128,4096]{1,0:T(8,128)(2,1)} %param.12) | copy-start | bytes 3145732
  246.8 9.4 %collective-permute-start = (bf16[128,1024]{1,0:T(8,128)(2,1)S(1)}, bf16[128,1024]{1,0:T(8,128)(2,1)S(1)}, u32[]{:S(2)}, u32[]{:S(2)}) collective-permute-start(bf16[128,1024]{1,0:T(8,128)(2,1)S(1)} %fusion.71), channel_id=1, source_target_pairs={{0,1},{1,2},{2,3},{3,4},{4,5},{5,6},{6,7},{8,9},{9,10},{10,11},{11... | collective-permute-start | bytes 786440 | tf_op jit(solution)/shard_map/while/body/eval_jaxpr/ppermute | solution.py:12
  264.5 9.5 %collective-permute-start = (bf16[128,1024]{1,0:T(8,128)(2,1)S(1)}, bf16[128,1024]{1,0:T(8,128)(2,1)S(1)}, u32[]{:S(2)}, u32[]{:S(2)}) collective-permute-start(bf16[128,1024]{1,0:T(8,128)(2,1)S(1)} %fusion.71), channel_id=1, source_target_pairs={{0,1},{1,2},{2,3},{3,4},{4,5},{5,6},{6,7},{8,9},{9,10},{10,11},{11... | collective-permute-start | bytes 786440 | tf_op jit(solution)/shard_map/while/body/eval_jaxpr/ppermute | solution.py:12
  282.4 8.6 %collective-permute-start = (bf16[128,1024]{1,0:T(8,128)(2,1)S(1)}, bf16[128,1024]{1,0:T(8,128)(2,1)S(1)}, u32[]{:S(2)}, u32[]{:S(2)}) collective-permute-start(bf16[128,1024]{1,0:T(8,128)(2,1)S(1)} %fusion.71), channel_id=1, source_target_pairs={{0,1},{1,2},{2,3},{3,4},{4,5},{5,6},{6,7},{8,9},{9,10},{10,11},{11... | collective-permute-start | bytes 786440 | tf_op jit(solution)/shard_map/while/body/eval_jaxpr/ppermute | solution.py:12
  299.3 8.3 %collective-permute-start = (bf16[128,1024]{1,0:T(8,128)(2,1)S(1)}, bf16[128,1024]{1,0:T(8,128)(2,1)S(1)}, u32[]{:S(2)}, u32[]{:S(2)}) collective-permute-start(bf16[128,1024]{1,0:T(8,128)(2,1)S(1)} %fusion.71), channel_id=1, source_target_pairs={{0,1},{1,2},{2,3},{3,4},{4,5},{5,6},{6,7},{8,9},{9,10},{10,11},{11... | collective-permute-start | bytes 786440 | tf_op jit(solution)/shard_map/while/body/eval_jaxpr/ppermute | solution.py:12
  315.9 8.3 %collective-permute-start = (bf16[128,1024]{1,0:T(8,128)(2,1)S(1)}, bf16[128,1024]{1,0:T(8,128)(2,1)S(1)}, u32[]{:S(2)}, u32[]{:S(2)}) collective-permute-start(bf16[128,1024]{1,0:T(8,128)(2,1)S(1)} %fusion.71), channel_id=1, source_target_pairs={{0,1},{1,2},{2,3},{3,4},{4,5},{5,6},{6,7},{8,9},{9,10},{10,11},{11... | collective-permute-start | bytes 786440 | tf_op jit(solution)/shard_map/while/body/eval_jaxpr/ppermute | solution.py:12
  332.5 8.3 %collective-permute-start = (bf16[128,1024]{1,0:T(8,128)(2,1)S(1)}, bf16[128,1024]{1,0:T(8,128)(2,1)S(1)}, u32[]{:S(2)}, u32[]{:S(2)}) collective-permute-start(bf16[128,1024]{1,0:T(8,128)(2,1)S(1)} %fusion.71), channel_id=1, source_target_pairs={{0,1},{1,2},{2,3},{3,4},{4,5},{5,6},{6,7},{8,9},{9,10},{10,11},{11... | collective-permute-start | bytes 786440 | tf_op jit(solution)/shard_map/while/body/eval_jaxpr/ppermute | solution.py:12
  349.1 10.3 %collective-permute-start = (bf16[128,1024]{1,0:T(8,128)(2,1)S(1)}, bf16[128,1024]{1,0:T(8,128)(2,1)S(1)}, u32[]{:S(2)}, u32[]{:S(2)}) collective-permute-start(bf16[128,1024]{1,0:T(8,128)(2,1)S(1)} %fusion.71), channel_id=1, source_target_pairs={{0,1},{1,2},{2,3},{3,4},{4,5},{5,6},{6,7},{8,9},{9,10},{10,11},{11... | collective-permute-start | bytes 786440 | tf_op jit(solution)/shard_map/while/body/eval_jaxpr/ppermute | solution.py:12
  365.7 133.5 %copy-start.5 = (bf16[128,1,1024]{2,0,1:T(8,128)(2,1)S(1)}, bf16[128,1,1024]{2,0,1:T(8,128)(2,1)}, u32[]{:S(2)}) copy-start(bf16[128,1,1024]{2,0,1:T(8,128)(2,1)} %param.19) | copy-start | bytes 786436
  374.2 10.8 %collective-permute-start.1 = (bf16[128,1024]{1,0:T(8,128)(2,1)S(1)}, bf16[128,1024]{1,0:T(8,128)(2,1)S(1)}, u32[]{:S(2)}, u32[]{:S(2)}) collective-permute-start(bf16[128,1024]{1,0:T(8,128)(2,1)S(1)} %add_convert_fusion.3), channel_id=1, source_target_pairs={{1,0},{2,1},{3,2},{4,3},{5,4},{6,5},{7,6},{9,8},{10,9},{11,10},{12... | collective-permute-start | bytes 786440 | tf_op jit(solution)/shard_map/while/body/eval_jaxpr/ppermute | solution.py:12
  393.4 10.8 %collective-permute-start.1 = (bf16[128,1024]{1,0:T(8,128)(2,1)S(1)}, bf16[128,1024]{1,0:T(8,128)(2,1)S(1)}, u32[]{:S(2)}, u32[]{:S(2)}) collective-permute-start(bf16[128,1024]{1,0:T(8,128)(2,1)S(1)} %add_convert_fusion.3), channel_id=1, source_target_pairs={{1,0},{2,1},{3,2},{4,3},{5,4},{6,5},{7,6},{9,8},{10,9},{11,10},{12... | collective-permute-start | bytes 786440 | tf_op jit(solution)/shard_map/while/body/eval_jaxpr/ppermute | solution.py:12
  412.7 10.8 %collective-permute-start.1 = (bf16[128,1024]{1,0:T(8,128)(2,1)S(1)}, bf16[128,1024]{1,0:T(8,128)(2,1)S(1)}, u32[]{:S(2)}, u32[]{:S(2)}) collective-permute-start(bf16[128,1024]{1,0:T(8,128)(2,1)S(1)} %add_convert_fusion.3), channel_id=1, source_target_pairs={{1,0},{2,1},{3,2},{4,3},{5,4},{6,5},{7,6},{9,8},{10,9},{11,10},{12... | collective-permute-start | bytes 786440 | tf_op jit(solution)/shard_map/while/body/eval_jaxpr/ppermute | solution.py:12
  431.9 10.8 %collective-permute-start.1 = (bf16[128,1024]{1,0:T(8,128)(2,1)S(1)}, bf16[128,1024]{1,0:T(8,128)(2,1)S(1)}, u32[]{:S(2)}, u32[]{:S(2)}) collective-permute-start(bf16[128,1024]{1,0:T(8,128)(2,1)S(1)} %add_convert_fusion.3), channel_id=1, source_target_pairs={{1,0},{2,1},{3,2},{4,3},{5,4},{6,5},{7,6},{9,8},{10,9},{11,10},{12... | collective-permute-start | bytes 786440 | tf_op jit(solution)/shard_map/while/body/eval_jaxpr/ppermute | solution.py:12
  451.2 10.4 %collective-permute-start.1 = (bf16[128,1024]{1,0:T(8,128)(2,1)S(1)}, bf16[128,1024]{1,0:T(8,128)(2,1)S(1)}, u32[]{:S(2)}, u32[]{:S(2)}) collective-permute-start(bf16[128,1024]{1,0:T(8,128)(2,1)S(1)} %add_convert_fusion.3), channel_id=1, source_target_pairs={{1,0},{2,1},{3,2},{4,3},{5,4},{6,5},{7,6},{9,8},{10,9},{11,10},{12... | collective-permute-start | bytes 786440 | tf_op jit(solution)/shard_map/while/body/eval_jaxpr/ppermute | solution.py:12
  470.0 10.4 %collective-permute-start.1 = (bf16[128,1024]{1,0:T(8,128)(2,1)S(1)}, bf16[128,1024]{1,0:T(8,128)(2,1)S(1)}, u32[]{:S(2)}, u32[]{:S(2)}) collective-permute-start(bf16[128,1024]{1,0:T(8,128)(2,1)S(1)} %add_convert_fusion.3), channel_id=1, source_target_pairs={{1,0},{2,1},{3,2},{4,3},{5,4},{6,5},{7,6},{9,8},{10,9},{11,10},{12... | collective-permute-start | bytes 786440 | tf_op jit(solution)/shard_map/while/body/eval_jaxpr/ppermute | solution.py:12
  488.8 10.4 %collective-permute-start.1 = (bf16[128,1024]{1,0:T(8,128)(2,1)S(1)}, bf16[128,1024]{1,0:T(8,128)(2,1)S(1)}, u32[]{:S(2)}, u32[]{:S(2)}) collective-permute-start(bf16[128,1024]{1,0:T(8,128)(2,1)S(1)} %add_convert_fusion.3), channel_id=1, source_target_pairs={{1,0},{2,1},{3,2},{4,3},{5,4},{6,5},{7,6},{9,8},{10,9},{11,10},{12... | collective-permute-start | bytes 786440 | tf_op jit(solution)/shard_map/while/body/eval_jaxpr/ppermute | solution.py:12
  504.6 5.6 copy-start.3
  515.8 190.3 %reduce-scatter.8.cloned.1.call-start = ((), (), s32[]{:S(2)}) async-start(), calls=%async_computation.3 | async-start | bytes 1179648 | tf_op jit(solution)/shard_map/reduce_scatter | solution.py:107
  523.1 256.8 %reduce-scatter.12.cloned.1.call-start = ((), (), s32[]{:S(2)}) async-start(), calls=%async_computation.5 | async-start | bytes 2228224 | tf_op jit(solution)/shard_map/reduce_scatter | solution.py:122
  526.0 3.3 copy-start.7
  532.7 134.9 %copy-start.6 = (u32[128]{0:T(128)S(1)}, u32[128]{0:T(128)}, u32[]{:S(2)}) copy-start(u32[128]{0:T(128)} %constant.72) | copy-start | bytes 1540
  532.7 247.2 %copy-start.1 = (bf16[1,1024,1024]{2,1,0:T(8,128)(2,1)S(1)}, bf16[1,1024,1024]{2,1,0:T(8,128)(2,1)}, u32[]{:S(2)}) copy-start(bf16[1,1024,1024]{2,1,0:T(8,128)(2,1)} %param.14) | copy-start | bytes 6291460
  651.1 17.9 %collective-permute-start.3 = (bf16[1024,60]{0,1:T(8,128)(2,1)S(1)}, bf16[1024,60]{0,1:T(8,128)(2,1)S(1)}, u32[]{:S(2)}, u32[]{:S(2)}) collective-permute-start(bf16[1024,60]{0,1:T(8,128)(2,1)S(1)} %slice.3), channel_id=1, source_target_pairs={{0,8},{8,16},{16,24},{24,32},{32,40},{40,48},{48,56},{56,64},{64,7... | collective-permute-start | bytes 368648
  661.1 8.1 %collective-permute-start.2 = (bf16[1024,60]{0,1:T(8,128)(2,1)S(1)}, bf16[1024,60]{0,1:T(8,128)(2,1)}, u32[]{:S(2)}, u32[]{:S(2)}) collective-permute-start(bf16[1024,60]{0,1:T(8,128)(2,1)S(1)} %slice.2), channel_id=1, source_target_pairs={{0,8},{8,16},{16,24},{24,32},{32,40},{40,48},{48,56},{56,64},{64,7... | collective-permute-start | bytes 368648
Sparse Core Ops, SparseCore 0:
  10.4 76.2 all-gather.8
  89.1 71.6 all-gather.10
  163.2 70.5 all-gather.6
  515.9 148.7 reduce-scatter.9
  667.5 38.5 reduce-scatter.7
  710.4 69.4 reduce-scatter.11
where the time goes:
time: 789 us; the launch traced here: 787 us
  waiting for transfers between devices  380 us (48%)
  matrix products  158 us (20%)
  blocking collectives  118 us (15%)
  starting transfers between devices  57.7 us (7%)
  local copies, waits for them, and re-layouts  53.7 us (7%)
  between operations  15 us (2%)
    dot_general x16, matrix products, contract_cols(): lax.dot_general(left, right, (((1,), (1,)), ((), ())), preferred_element_...  127 us
    unnamed x1, blocking collectives  118 us
    ppermute x14, waiting for transfers between devices, shifted(): return lax.ppermute(block, axis, route)  96.1 us
    reduce_scatter x1, waiting for transfers between devices, per_device(): lax.psum_scatter(contract_rows(onehot, carried).astype(jnp.bfloat16), 'dp...  73.9 us
    all_gather x1, waiting for transfers between devices, per_device(): lax.all_gather(depth_w1[0], 'dp', axis=1, tiled=True)  71.7 us
    all_gather x1, waiting for transfers between devices, per_device(): lax.all_gather(depth_w2[0], 'dp', axis=1, tiled=True)  53.2 us
    all_gather x1, waiting for transfers between devices, per_device(): projection = lax.all_gather(depth_in[0], 'dp', axis=0, tiled=True)  52.1 us
    unnamed x26, local copies, waits for them, and re-layouts  50.6 us
  transfers between devices with their start and end apart: 22, of which 19 were waited for; matrix products, arithmetic and copies ran while one was open for 24% of the time, Pallas kernels for 0%

commit v1 on v0

--- a/solution.py
+++ b/solution.py
@@ -36,6 +36,12 @@
 def per_device(
     temporal_out, depth_in, embed, depth_w1, depth_w2, audio_tokens, barge_mask, out_grad
 ):
+
+    def solve_trees(sheet, link_axis):
+        response = jnp.stack([sheet for _ in range(lax.axis_size(link_axis))])
+        side_arr = lax.all_to_all(response, link_axis, split_axis=0, concat_axis=0)
+        return jnp.concatenate(side_arr, axis=1)
+
     dp_index = lax.axis_index("dp")
     n_code = lax.axis_size("code")
     own_rows = temporal_out.shape[0]
@@ -48,7 +54,7 @@
     )
     width_depth = depth_base.shape[1]
     w_first, w_second = (
-        lax.all_gather(depth_w1[0], "dp", axis=1, tiled=True),
+        solve_trees(depth_w1[0], "dp"),
         lax.all_gather(depth_w2[0], "dp", axis=1, tiled=True),
     )
 

time: 789 us -> 754 us (0.956)
  waiting for transfers between devices: 380 us -> 349 us
    all_to_all x0 -> x1, waiting for transfers between devices: none -> 73.9 us  [solve_trees(): side_arr = lax.all_to_all(response, link_axis, split_axis=0, concat_axis=0)]
    all_gather x1 -> x0, waiting for transfers between devices: 71.7 us -> none  [per_device(): lax.all_gather(depth_w1[0], 'dp', axis=1, tiled=True)]
    all_gather x1, waiting for transfers between devices: 53.2 us -> 13.7 us  [per_device(): lax.all_gather(depth_w2[0], 'dp', axis=1, tiled=True)]
    unnamed x26, local copies, waits for them, and re-layouts: 50.6 us -> 27.5 us
where the time goes in v1:
time: 754 us; the launch traced here: 753 us
  waiting for transfers between devices  349 us (46%)
  matrix products  154 us (20%)
  blocking collectives  118 us (16%)
  starting transfers between devices  65.1 us (9%)
  local copies, waits for them, and re-layouts  47.6 us (6%)
  between operations  14.6 us (2%)
    dot_general x16, matrix products, contract_cols(): lax.dot_general(left, right, (((1,), (1,)), ((), ())), preferred_element_...  125 us
    unnamed x1, blocking collectives  118 us
    ppermute x14, waiting for transfers between devices, shifted(): return lax.ppermute(block, axis, route)  96.1 us
    all_to_all x1, waiting for transfers between devices, solve_trees(): side_arr = lax.all_to_all(response, link_axis, split_axis=0, concat_axis=0)  73.9 us
    reduce_scatter x1, waiting for transfers between devices, per_device(): lax.psum_scatter(contract_rows(onehot, carried).astype(jnp.bfloat16), 'dp...  73.8 us
    all_gather x1, waiting for transfers between devices, per_device(): projection = lax.all_gather(depth_in[0], 'dp', axis=0, tiled=True)  58.9 us
    ppermute x14, starting transfers between devices, shifted(): return lax.ppermute(block, axis, route)  40.9 us
    reduce_scatter x1, waiting for transfers between devices, per_device(): lax.psum_scatter(contract_cols(carried, projection).astype(jnp.bfloat16),...  31.9 us
  transfers between devices with their start and end apart: 22, of which 19 were waited for; matrix products, arithmetic and copies ran while one was open for 24% of the time, Pallas kernels for 0%

profile of v1, /device:TPU:0, one launch (start us, length us, event | category | flops | bytes accessed | tf_op | source)
XLA Modules:
  0.0 752.7 jit_solution(6084625210522888029)
XLA Ops:
  7.2 2.3 copy.28
  10.3 3.6 stack.3
  13.9 7.3 all-to-all-start
  23.0 73.9 %all-to-all-done = bf16[16,1024,132]{1,2,0:T(8,128)(2,1)} async-done(((bf16[16,1024,132]{1,2,0:T(8,128)(2,1)}), bf16[16,1024,132]{1,2,0:T(8,128)(2,1)}, u32[]{:S(2)}, u32[]{:S(2)}) %all-to-all-start) | async-done | bytes 4325408 | tf_op jit(solution)/shard_map/all_to_all | solution.py:42
  96.9 7.0 reshape.64
  103.9 6.4 copy.29
  110.3 13.7 %all-gather.7.cloned.1.call-done = bf16[1,1024,2112]{1,0,2:T(2,128)(2,1)} async-done(((bf16[1,1024,132]{1,0,2:T(2,128)(2,1)}), bf16[1,1024,2112]{1,0,2:T(2,128)(2,1)}) %all-gather.7.cloned.1.call-update) | async-done | bytes 4325392 | tf_op jit(solution)/shard_map/all_gather | solution.py:58
  123.9 20.8 %copy.35 = bf16[1,1024,2112]{2,1,0:T(8,128)(2,1)} copy(bf16[1,1024,2112]{1,0,2:T(2,128)(2,1)} %all-gather.7.cloned.1.call-done) | data formatting | bytes 8650752
  144.8 58.9 %all-gather.5.cloned.1.call-done = bf16[1,4096,1024]{2,1,0:T(8,128)(2,1)} async-done(((bf16[1,256,1024]{2,1,0:T(8,128)(2,1)}), bf16[1,4096,1024]{2,1,0:T(8,128)(2,1)}) %all-gather.5.cloned.1.call-update) | async-done | bytes 8388624 | tf_op jit(solution)/shard_map/all_gather | solution.py:48
  203.6 4.6 fusion.29
  208.3 120.9 %while.20 = (s32[]{:T(128)}, bf16[128,1024]{1,0:T(8,128)(2,1)S(1)}, f32[128,1024]{1,0:T(8,128)S(1)}, bf16[1024,2112]{1,0:T(8,128)(2,1)}, bf16[1024,2112]{1,0:T(8,128)(2,1)}, /*index=5*/s32[]{:T(128)}) while((s32[]{:T(128)}, bf16[128,1024]{1,0:T(8,128)(2,1)S(1)}, f32[128,1024]{1,0:T(8,128)S(1)}, bf16[1024,2112]{1,0:T(8,128)(2,1)}, ...), condition=%wide.region_2.3_spmd, body=%wide.region_0.0_spmd.sunk | while | flops 1110220928 | bytes 11536493 | solution.py:75
  208.5 8.2 %fusion.68 = bf16[128,1024]{1,0:T(8,128)(2,1)S(1)} fusion(bf16[1024,2112]{1,0:T(8,128)(2,1)} %get-tuple-element.283, bf16[1024,2112]{1,0:T(8,128)(2,1)} %get-tuple-element.282, f32[128,1024]{1,0:T(8,128)S(1)} %get-tuple-element.281, bf16[128,1024]{1,0:T(8,128)(2,1)S(1)} %get-tuple-element.274, f32[128]{0:T(128)S(1)} %add_rsqrt_fusion.3), kind=kOutput, calls=%fused_computation.2.clone.1 | convolution fusion | flops 1109696512 | bytes 9699840 | tf_op jit(solution)/shard_map/while/body/eval_jaxpr/dot_general | solution.py:26
  216.7 3.5 collective-permute-start
  220.1 5.9 collective-permute-done
  226.2 8.2 %fusion.68 = bf16[128,1024]{1,0:T(8,128)(2,1)S(1)} fusion(bf16[1024,2112]{1,0:T(8,128)(2,1)} %get-tuple-element.283, bf16[1024,2112]{1,0:T(8,128)(2,1)} %get-tuple-element.282, f32[128,1024]{1,0:T(8,128)S(1)} %get-tuple-element.281, bf16[128,1024]{1,0:T(8,128)(2,1)S(1)} %get-tuple-element.274, f32[128]{0:T(128)S(1)} %add_rsqrt_fusion.3), kind=kOutput, calls=%fused_computation.2.clone.1 | convolution fusion | flops 1109696512 | bytes 9699840 | tf_op jit(solution)/shard_map/while/body/eval_jaxpr/dot_general | solution.py:26
  234.4 4.4 collective-permute-start
  238.8 5.1 collective-permute-done
  244.1 8.2 %fusion.68 = bf16[128,1024]{1,0:T(8,128)(2,1)S(1)} fusion(bf16[1024,2112]{1,0:T(8,128)(2,1)} %get-tuple-element.283, bf16[1024,2112]{1,0:T(8,128)(2,1)} %get-tuple-element.282, f32[128,1024]{1,0:T(8,128)S(1)} %get-tuple-element.281, bf16[128,1024]{1,0:T(8,128)(2,1)S(1)} %get-tuple-element.274, f32[128]{0:T(128)S(1)} %add_rsqrt_fusion.3), kind=kOutput, calls=%fused_computation.2.clone.1 | convolution fusion | flops 1109696512 | bytes 9699840 | tf_op jit(solution)/shard_map/while/body/eval_jaxpr/dot_general | solution.py:26
  252.3 4.4 collective-permute-start
  256.7 4.2 collective-permute-done
  261.0 8.2 %fusion.68 = bf16[128,1024]{1,0:T(8,128)(2,1)S(1)} fusion(bf16[1024,2112]{1,0:T(8,128)(2,1)} %get-tuple-element.283, bf16[1024,2112]{1,0:T(8,128)(2,1)} %get-tuple-element.282, f32[128,1024]{1,0:T(8,128)S(1)} %get-tuple-element.281, bf16[128,1024]{1,0:T(8,128)(2,1)S(1)} %get-tuple-element.274, f32[128]{0:T(128)S(1)} %add_rsqrt_fusion.3), kind=kOutput, calls=%fused_computation.2.clone.1 | convolution fusion | flops 1109696512 | bytes 9699840 | tf_op jit(solution)/shard_map/while/body/eval_jaxpr/dot_general | solution.py:26
  269.2 4.4 collective-permute-start
  273.6 3.9 collective-permute-done
  277.6 8.2 %fusion.68 = bf16[128,1024]{1,0:T(8,128)(2,1)S(1)} fusion(bf16[1024,2112]{1,0:T(8,128)(2,1)} %get-tuple-element.283, bf16[1024,2112]{1,0:T(8,128)(2,1)} %get-tuple-element.282, f32[128,1024]{1,0:T(8,128)S(1)} %get-tuple-element.281, bf16[128,1024]{1,0:T(8,128)(2,1)S(1)} %get-tuple-element.274, f32[128]{0:T(128)S(1)} %add_rsqrt_fusion.3), kind=kOutput, calls=%fused_computation.2.clone.1 | convolution fusion | flops 1109696512 | bytes 9699840 | tf_op jit(solution)/shard_map/while/body/eval_jaxpr/dot_general | solution.py:26
  285.8 4.4 collective-permute-start
  290.2 3.9 collective-permute-done
  294.2 8.2 %fusion.68 = bf16[128,1024]{1,0:T(8,128)(2,1)S(1)} fusion(bf16[1024,2112]{1,0:T(8,128)(2,1)} %get-tuple-element.283, bf16[1024,2112]{1,0:T(8,128)(2,1)} %get-tuple-element.282, f32[128,1024]{1,0:T(8,128)S(1)} %get-tuple-element.281, bf16[128,1024]{1,0:T(8,128)(2,1)S(1)} %get-tuple-element.274, f32[128]{0:T(128)S(1)} %add_rsqrt_fusion.3), kind=kOutput, calls=%fused_computation.2.clone.1 | convolution fusion | flops 1109696512 | bytes 9699840 | tf_op jit(solution)/shard_map/while/body/eval_jaxpr/dot_general | solution.py:26
  302.4 4.4 collective-permute-start
  306.8 3.9 collective-permute-done
  310.8 8.2 %fusion.68 = bf16[128,1024]{1,0:T(8,128)(2,1)S(1)} fusion(bf16[1024,2112]{1,0:T(8,128)(2,1)} %get-tuple-element.283, bf16[1024,2112]{1,0:T(8,128)(2,1)} %get-tuple-element.282, f32[128,1024]{1,0:T(8,128)S(1)} %get-tuple-element.281, bf16[128,1024]{1,0:T(8,128)(2,1)S(1)} %get-tuple-element.274, f32[128]{0:T(128)S(1)} %add_rsqrt_fusion.3), kind=kOutput, calls=%fused_computation.2.clone.1 | convolution fusion | flops 1109696512 | bytes 9699840 | tf_op jit(solution)/shard_map/while/body/eval_jaxpr/dot_general | solution.py:26
  319.0 6.4 collective-permute-start
  325.4 3.9 collective-permute-done
  329.5 4.5 add_multiply_fusion
  334.1 133.4 %while.21 = (s32[]{:T(128)}, bf16[128,1024]{1,0:T(8,128)(2,1)S(1)}, f32[128,1024]{1,0:T(8,128)S(1)}, f32[128,1]{0,1:T(1,128)S(1)}, bf16[1024,2112]{1,0:T(8,128)(...) while((s32[]{:T(128)}, bf16[128,1024]{1,0:T(8,128)(2,1)S(1)}, ...), condition=%wide.region_6.7_spmd, body=%wide.region_4.6_spmd.sunk | while | flops 1109409792 | bytes 14715525 | solution.py:97
  334.1 8.2 %multiply_reduce_fusion.7 = (f32[128]{0:T(128)S(1)}, f32[128,1024]{1,0:T(8,128)S(1)}) fusion(f32[128,1024]{1,0:T(8,128)S(1)} %get-tuple-element.310, bf16[1024,2112]{1,0:T(8,128)(2,1)} %get-tuple-element.309, f32[128,2112]{0,1:T(8,128)S(1)} %get-tuple-element.308, bf16[1024,2112]{1,0:T(8,128)(2,1)} %get-tuple-element.307, ...), kind=kOutput, calls=%fused_computation.16.clone.1 | convolution fusion | flops 1108492160 | bytes 11567616 | tf_op jit(solution)/shard_map/while/body/eval_jaxpr/dot_general | solution.py:26
  342.5 1.3 collective-permute-start.1
  343.8 9.5 %collective-permute-done.1 = bf16[128,1024]{1,0:T(8,128)(2,1)S(1)} collective-permute-done((bf16[128,1024]{1,0:T(8,128)(2,1)S(1)}, bf16[128,1024]{1,0:T(8,128)(2,1)S(1)}, u32[]{:S(2)}, u32[]{:S(2)}) %collective-permute-start.1) | collective-permute-done | bytes 262176 | tf_op jit(solution)/shard_map/while/body/eval_jaxpr/ppermute | solution.py:12
  353.4 8.2 %multiply_reduce_fusion.7 = (f32[128]{0:T(128)S(1)}, f32[128,1024]{1,0:T(8,128)S(1)}) fusion(f32[128,1024]{1,0:T(8,128)S(1)} %get-tuple-element.310, bf16[1024,2112]{1,0:T(8,128)(2,1)} %get-tuple-element.309, f32[128,2112]{0,1:T(8,128)S(1)} %get-tuple-element.308, bf16[1024,2112]{1,0:T(8,128)(2,1)} %get-tuple-element.307, ...), kind=kOutput, calls=%fused_computation.16.clone.1 | convolution fusion | flops 1108492160 | bytes 11567616 | tf_op jit(solution)/shard_map/while/body/eval_jaxpr/dot_general | solution.py:26
  361.8 1.3 collective-permute-start.1
  363.1 9.5 %collective-permute-done.1 = bf16[128,1024]{1,0:T(8,128)(2,1)S(1)} collective-permute-done((bf16[128,1024]{1,0:T(8,128)(2,1)S(1)}, bf16[128,1024]{1,0:T(8,128)(2,1)S(1)}, u32[]{:S(2)}, u32[]{:S(2)}) %collective-permute-start.1) | collective-permute-done | bytes 262176 | tf_op jit(solution)/shard_map/while/body/eval_jaxpr/ppermute | solution.py:12
  372.6 8.2 %multiply_reduce_fusion.7 = (f32[128]{0:T(128)S(1)}, f32[128,1024]{1,0:T(8,128)S(1)}) fusion(f32[128,1024]{1,0:T(8,128)S(1)} %get-tuple-element.310, bf16[1024,2112]{1,0:T(8,128)(2,1)} %get-tuple-element.309, f32[128,2112]{0,1:T(8,128)S(1)} %get-tuple-element.308, bf16[1024,2112]{1,0:T(8,128)(2,1)} %get-tuple-element.307, ...), kind=kOutput, calls=%fused_computation.16.clone.1 | convolution fusion | flops 1108492160 | bytes 11567616 | tf_op jit(solution)/shard_map/while/body/eval_jaxpr/dot_general | solution.py:26
  382.3 9.5 %collective-permute-done.1 = bf16[128,1024]{1,0:T(8,128)(2,1)S(1)} collective-permute-done((bf16[128,1024]{1,0:T(8,128)(2,1)S(1)}, bf16[128,1024]{1,0:T(8,128)(2,1)S(1)}, u32[]{:S(2)}, u32[]{:S(2)}) %collective-permute-start.1) | collective-permute-done | bytes 262176 | tf_op jit(solution)/shard_map/while/body/eval_jaxpr/ppermute | solution.py:12
  391.9 8.2 %multiply_reduce_fusion.7 = (f32[128]{0:T(128)S(1)}, f32[128,1024]{1,0:T(8,128)S(1)}) fusion(f32[128,1024]{1,0:T(8,128)S(1)} %get-tuple-element.310, bf16[1024,2112]{1,0:T(8,128)(2,1)} %get-tuple-element.309, f32[128,2112]{0,1:T(8,128)S(1)} %get-tuple-element.308, bf16[1024,2112]{1,0:T(8,128)(2,1)} %get-tuple-element.307, ...), kind=kOutput, calls=%fused_computation.16.clone.1 | convolution fusion | flops 1108492160 | bytes 11567616 | tf_op jit(solution)/shard_map/while/body/eval_jaxpr/dot_general | solution.py:26
  401.6 9.5 %collective-permute-done.1 = bf16[128,1024]{1,0:T(8,128)(2,1)S(1)} collective-permute-done((bf16[128,1024]{1,0:T(8,128)(2,1)S(1)}, bf16[128,1024]{1,0:T(8,128)(2,1)S(1)}, u32[]{:S(2)}, u32[]{:S(2)}) %collective-permute-start.1) | collective-permute-done | bytes 262176 | tf_op jit(solution)/shard_map/while/body/eval_jaxpr/ppermute | solution.py:12
  411.1 8.2 %multiply_reduce_fusion.7 = (f32[128]{0:T(128)S(1)}, f32[128,1024]{1,0:T(8,128)S(1)}) fusion(f32[128,1024]{1,0:T(8,128)S(1)} %get-tuple-element.310, bf16[1024,2112]{1,0:T(8,128)(2,1)} %get-tuple-element.309, f32[128,2112]{0,1:T(8,128)S(1)} %get-tuple-element.308, bf16[1024,2112]{1,0:T(8,128)(2,1)} %get-tuple-element.307, ...), kind=kOutput, calls=%fused_computation.16.clone.1 | convolution fusion | flops 1108492160 | bytes 11567616 | tf_op jit(solution)/shard_map/while/body/eval_jaxpr/dot_general | solution.py:26
  420.8 9.1 %collective-permute-done.1 = bf16[128,1024]{1,0:T(8,128)(2,1)S(1)} collective-permute-done((bf16[128,1024]{1,0:T(8,128)(2,1)S(1)}, bf16[128,1024]{1,0:T(8,128)(2,1)S(1)}, u32[]{:S(2)}, u32[]{:S(2)}) %collective-permute-start.1) | collective-permute-done | bytes 262176 | tf_op jit(solution)/shard_map/while/body/eval_jaxpr/ppermute | solution.py:12
  429.9 8.2 %multiply_reduce_fusion.7 = (f32[128]{0:T(128)S(1)}, f32[128,1024]{1,0:T(8,128)S(1)}) fusion(f32[128,1024]{1,0:T(8,128)S(1)} %get-tuple-element.310, bf16[1024,2112]{1,0:T(8,128)(2,1)} %get-tuple-element.309, f32[128,2112]{0,1:T(8,128)S(1)} %get-tuple-element.308, bf16[1024,2112]{1,0:T(8,128)(2,1)} %get-tuple-element.307, ...), kind=kOutput, calls=%fused_computation.16.clone.1 | convolution fusion | flops 1108492160 | bytes 11567616 | tf_op jit(solution)/shard_map/while/body/eval_jaxpr/dot_general | solution.py:26
  439.6 9.1 %collective-permute-done.1 = bf16[128,1024]{1,0:T(8,128)(2,1)S(1)} collective-permute-done((bf16[128,1024]{1,0:T(8,128)(2,1)S(1)}, bf16[128,1024]{1,0:T(8,128)(2,1)S(1)}, u32[]{:S(2)}, u32[]{:S(2)}) %collective-permute-start.1) | collective-permute-done | bytes 262176 | tf_op jit(solution)/shard_map/while/body/eval_jaxpr/ppermute | solution.py:12
  448.7 8.2 %multiply_reduce_fusion.7 = (f32[128]{0:T(128)S(1)}, f32[128,1024]{1,0:T(8,128)S(1)}) fusion(f32[128,1024]{1,0:T(8,128)S(1)} %get-tuple-element.310, bf16[1024,2112]{1,0:T(8,128)(2,1)} %get-tuple-element.309, f32[128,2112]{0,1:T(8,128)S(1)} %get-tuple-element.308, bf16[1024,2112]{1,0:T(8,128)(2,1)} %get-tuple-element.307, ...), kind=kOutput, calls=%fused_computation.16.clone.1 | convolution fusion | flops 1108492160 | bytes 11567616 | tf_op jit(solution)/shard_map/while/body/eval_jaxpr/dot_general | solution.py:26
  457.1 1.3 collective-permute-start.1
  458.4 9.1 %collective-permute-done.1 = bf16[128,1024]{1,0:T(8,128)(2,1)S(1)} collective-permute-done((bf16[128,1024]{1,0:T(8,128)(2,1)S(1)}, bf16[128,1024]{1,0:T(8,128)(2,1)S(1)}, u32[]{:S(2)}, u32[]{:S(2)}) %collective-permute-start.1) | collective-permute-done | bytes 262176 | tf_op jit(solution)/shard_map/while/body/eval_jaxpr/ppermute | solution.py:12
  467.5 5.4 fusion.26
  473.0 3.2 multiply_reduce_fusion.2
  476.5 5.6 convert_bitcast_fusion
  482.1 7.3 fusion.17
  490.1 2.2 convolution_convert_fusion.2
  492.3 3.3 convolution_convert_fusion.1
  495.6 3.4 convolution_convert_fusion
  499.0 118.2 %fusion.44 = (bf16[1024,136]{0,1:T(8,128)(2,1)S(1)}, bf16[1024,136]{0,1:T(8,128)(2,1)S(1)}) fusion(bf16[1024,2112]{0,1:T(8,128)(2,1)} %convolution_convert_fusion.1, bf16[1024,2112]{0,1:T(8,128)(2,1)} %convolution_convert_fusion), kind=kCustom, calls=%all-reduce-scatter.2 | all-reduce-scatter fusion | flops 4456449 | bytes 9208320
  617.3 10.1 %collective-permute-start.3 = (bf16[1024,60]{0,1:T(8,128)(2,1)S(1)}, bf16[1024,60]{0,1:T(8,128)(2,1)S(1)}, u32[]{:S(2)}, u32[]{:S(2)}) collective-permute-start(bf16[1024,60]{0,1:T(8,128)(2,1)S(1)} %slice.3), channel_id=1, source_target_pairs={{0,8},{8,16},{16,24},{24,32},{32,40},{40,48},{48,56},{56,64},{64,7... | collective-permute-start | bytes 368648
  627.5 6.5 collective-permute-start.2
  638.4 2.0 copy.33
  640.5 31.9 %reduce-scatter.8.cloned.1.call-done = bf16[128,512]{1,0:T(8,128)(2,1)} async-done(((bf16[128,4096]{1,0:T(8,128)(2,1)}), bf16[128,512]{1,0:T(8,128)(2,1)}) %reduce-scatter.8.cloned.1.call-update) | async-done | bytes 131088 | tf_op jit(solution)/shard_map/reduce_scatter | solution.py:113
  672.4 73.8 %reduce-scatter.12.cloned.1.call-done = bf16[64,1024]{1,0:T(8,128)(2,1)} async-done(((bf16[1024,1024]{1,0:T(8,128)(2,1)}), bf16[64,1024]{1,0:T(8,128)(2,1)}) %reduce-scatter.12.cloned.1.call-update) | async-done | bytes 131088 | tf_op jit(solution)/shard_map/reduce_scatter | solution.py:128
  (83 shorter events, 15.3 us)
Async XLA Ops:
  7.2 14.8 %copy-start = (bf16[1,1024,1024]{2,1,0:T(8,128)(2,1)S(1)}, bf16[1,1024,1024]{2,1,0:T(8,128)(2,1)}, u32[]{:S(2)}) copy-start(bf16[1,1024,1024]{2,1,0:T(8,128)(2,1)} %param.14) | copy-start | bytes 6291460
  7.2 116.7 %all-gather.7.cloned.1.call-start = ((), (), s32[]{:S(2)}) async-start(), calls=%async_computation.8 | async-start | bytes 9191424 | tf_op jit(solution)/shard_map/all_gather | solution.py:58
  9.6 194.1 %all-gather.5.cloned.1.call-start = ((), (), s32[]{:S(2)}) async-start(), calls=%async_computation.7 | async-start | bytes 8912896 | tf_op jit(solution)/shard_map/all_gather | solution.py:48
  13.9 7.4 copy-start.7
  13.9 8.9 %copy-start.4 = (bf16[128,1,1024]{2,0,1:T(8,128)(2,1)S(1)}, bf16[128,1,1024]{2,0,1:T(8,128)(2,1)}, u32[]{:S(2)}) copy-start(bf16[128,1,1024]{2,0,1:T(8,128)(2,1)} %param.19) | copy-start | bytes 786436
  13.9 82.9 %all-to-all-start = ((bf16[16,1024,132]{1,2,0:T(8,128)(2,1)}), bf16[16,1024,132]{1,2,0:T(8,128)(2,1)}, u32[]{:S(2)}, u32[]{:S(2)}) async-start(bf16[16,1024,132]{1,2,0:T(8,128)(2,1)} %stack.3), calls=%async_computation | async-start | bytes 8912896 | tf_op jit(solution)/shard_map/all_to_all | solution.py:42
  21.2 617.2 %reduce-scatter.10.cloned.1.call-start = ((), (), s32[]{:S(2)}) async-start(), calls=%async_computation.5 | async-start | bytes 8912896 | tf_op jit(solution)/shard_map/reduce_scatter | solution.py:122
  110.3 93.4 %copy-start.2 = (bf16[128,4096]{1,0:T(8,128)(2,1)S(1)}, bf16[128,4096]{1,0:T(8,128)(2,1)}, u32[]{:S(2)}) copy-start(bf16[128,4096]{1,0:T(8,128)(2,1)} %param.12) | copy-start | bytes 3145732
  216.7 9.4 %collective-permute-start = (bf16[128,1024]{1,0:T(8,128)(2,1)S(1)}, bf16[128,1024]{1,0:T(8,128)(2,1)S(1)}, u32[]{:S(2)}, u32[]{:S(2)}) collective-permute-start(bf16[128,1024]{1,0:T(8,128)(2,1)S(1)} %fusion.68), channel_id=1, source_target_pairs={{0,1},{1,2},{2,3},{3,4},{4,5},{5,6},{6,7},{8,9},{9,10},{10,11},{11... | collective-permute-start | bytes 786440 | tf_op jit(solution)/shard_map/while/body/eval_jaxpr/ppermute | solution.py:12
  234.4 9.5 %collective-permute-start = (bf16[128,1024]{1,0:T(8,128)(2,1)S(1)}, bf16[128,1024]{1,0:T(8,128)(2,1)S(1)}, u32[]{:S(2)}, u32[]{:S(2)}) collective-permute-start(bf16[128,1024]{1,0:T(8,128)(2,1)S(1)} %fusion.68), channel_id=1, source_target_pairs={{0,1},{1,2},{2,3},{3,4},{4,5},{5,6},{6,7},{8,9},{9,10},{10,11},{11... | collective-permute-start | bytes 786440 | tf_op jit(solution)/shard_map/while/body/eval_jaxpr/ppermute | solution.py:12
  252.3 8.6 %collective-permute-start = (bf16[128,1024]{1,0:T(8,128)(2,1)S(1)}, bf16[128,1024]{1,0:T(8,128)(2,1)S(1)}, u32[]{:S(2)}, u32[]{:S(2)}) collective-permute-start(bf16[128,1024]{1,0:T(8,128)(2,1)S(1)} %fusion.68), channel_id=1, source_target_pairs={{0,1},{1,2},{2,3},{3,4},{4,5},{5,6},{6,7},{8,9},{9,10},{10,11},{11... | collective-permute-start | bytes 786440 | tf_op jit(solution)/shard_map/while/body/eval_jaxpr/ppermute | solution.py:12
  269.2 8.3 %collective-permute-start = (bf16[128,1024]{1,0:T(8,128)(2,1)S(1)}, bf16[128,1024]{1,0:T(8,128)(2,1)S(1)}, u32[]{:S(2)}, u32[]{:S(2)}) collective-permute-start(bf16[128,1024]{1,0:T(8,128)(2,1)S(1)} %fusion.68), channel_id=1, source_target_pairs={{0,1},{1,2},{2,3},{3,4},{4,5},{5,6},{6,7},{8,9},{9,10},{10,11},{11... | collective-permute-start | bytes 786440 | tf_op jit(solution)/shard_map/while/body/eval_jaxpr/ppermute | solution.py:12
  285.8 8.3 %collective-permute-start = (bf16[128,1024]{1,0:T(8,128)(2,1)S(1)}, bf16[128,1024]{1,0:T(8,128)(2,1)S(1)}, u32[]{:S(2)}, u32[]{:S(2)}) collective-permute-start(bf16[128,1024]{1,0:T(8,128)(2,1)S(1)} %fusion.68), channel_id=1, source_target_pairs={{0,1},{1,2},{2,3},{3,4},{4,5},{5,6},{6,7},{8,9},{9,10},{10,11},{11... | collective-permute-start | bytes 786440 | tf_op jit(solution)/shard_map/while/body/eval_jaxpr/ppermute | solution.py:12
  302.4 8.3 %collective-permute-start = (bf16[128,1024]{1,0:T(8,128)(2,1)S(1)}, bf16[128,1024]{1,0:T(8,128)(2,1)S(1)}, u32[]{:S(2)}, u32[]{:S(2)}) collective-permute-start(bf16[128,1024]{1,0:T(8,128)(2,1)S(1)} %fusion.68), channel_id=1, source_target_pairs={{0,1},{1,2},{2,3},{3,4},{4,5},{5,6},{6,7},{8,9},{9,10},{10,11},{11... | collective-permute-start | bytes 786440 | tf_op jit(solution)/shard_map/while/body/eval_jaxpr/ppermute | solution.py:12
  319.0 10.3 %collective-permute-start = (bf16[128,1024]{1,0:T(8,128)(2,1)S(1)}, bf16[128,1024]{1,0:T(8,128)(2,1)S(1)}, u32[]{:S(2)}, u32[]{:S(2)}) collective-permute-start(bf16[128,1024]{1,0:T(8,128)(2,1)S(1)} %fusion.68), channel_id=1, source_target_pairs={{0,1},{1,2},{2,3},{3,4},{4,5},{5,6},{6,7},{8,9},{9,10},{10,11},{11... | collective-permute-start | bytes 786440 | tf_op jit(solution)/shard_map/while/body/eval_jaxpr/ppermute | solution.py:12
  334.1 133.5 %copy-start.5 = (bf16[128,1,1024]{2,0,1:T(8,128)(2,1)S(1)}, bf16[128,1,1024]{2,0,1:T(8,128)(2,1)}, u32[]{:S(2)}) copy-start(bf16[128,1,1024]{2,0,1:T(8,128)(2,1)} %param.19) | copy-start | bytes 786436
  342.5 10.8 %collective-permute-start.1 = (bf16[128,1024]{1,0:T(8,128)(2,1)S(1)}, bf16[128,1024]{1,0:T(8,128)(2,1)S(1)}, u32[]{:S(2)}, u32[]{:S(2)}) collective-permute-start(bf16[128,1024]{1,0:T(8,128)(2,1)S(1)} %add_convert_fusion.3), channel_id=1, source_target_pairs={{1,0},{2,1},{3,2},{4,3},{5,4},{6,5},{7,6},{9,8},{10,9},{11,10},{12... | collective-permute-start | bytes 786440 | tf_op jit(solution)/shard_map/while/body/eval_jaxpr/ppermute | solution.py:12
  361.8 10.8 %collective-permute-start.1 = (bf16[128,1024]{1,0:T(8,128)(2,1)S(1)}, bf16[128,1024]{1,0:T(8,128)(2,1)S(1)}, u32[]{:S(2)}, u32[]{:S(2)}) collective-permute-start(bf16[128,1024]{1,0:T(8,128)(2,1)S(1)} %add_convert_fusion.3), channel_id=1, source_target_pairs={{1,0},{2,1},{3,2},{4,3},{5,4},{6,5},{7,6},{9,8},{10,9},{11,10},{12... | collective-permute-start | bytes 786440 | tf_op jit(solution)/shard_map/while/body/eval_jaxpr/ppermute | solution.py:12
  381.0 10.8 %collective-permute-start.1 = (bf16[128,1024]{1,0:T(8,128)(2,1)S(1)}, bf16[128,1024]{1,0:T(8,128)(2,1)S(1)}, u32[]{:S(2)}, u32[]{:S(2)}) collective-permute-start(bf16[128,1024]{1,0:T(8,128)(2,1)S(1)} %add_convert_fusion.3), channel_id=1, source_target_pairs={{1,0},{2,1},{3,2},{4,3},{5,4},{6,5},{7,6},{9,8},{10,9},{11,10},{12... | collective-permute-start | bytes 786440 | tf_op jit(solution)/shard_map/while/body/eval_jaxpr/ppermute | solution.py:12
  400.3 10.8 %collective-permute-start.1 = (bf16[128,1024]{1,0:T(8,128)(2,1)S(1)}, bf16[128,1024]{1,0:T(8,128)(2,1)S(1)}, u32[]{:S(2)}, u32[]{:S(2)}) collective-permute-start(bf16[128,1024]{1,0:T(8,128)(2,1)S(1)} %add_convert_fusion.3), channel_id=1, source_target_pairs={{1,0},{2,1},{3,2},{4,3},{5,4},{6,5},{7,6},{9,8},{10,9},{11,10},{12... | collective-permute-start | bytes 786440 | tf_op jit(solution)/shard_map/while/body/eval_jaxpr/ppermute | solution.py:12
  419.5 10.4 %collective-permute-start.1 = (bf16[128,1024]{1,0:T(8,128)(2,1)S(1)}, bf16[128,1024]{1,0:T(8,128)(2,1)S(1)}, u32[]{:S(2)}, u32[]{:S(2)}) collective-permute-start(bf16[128,1024]{1,0:T(8,128)(2,1)S(1)} %add_convert_fusion.3), channel_id=1, source_target_pairs={{1,0},{2,1},{3,2},{4,3},{5,4},{6,5},{7,6},{9,8},{10,9},{11,10},{12... | collective-permute-start | bytes 786440 | tf_op jit(solution)/shard_map/while/body/eval_jaxpr/ppermute | solution.py:12
  438.3 10.4 %collective-permute-start.1 = (bf16[128,1024]{1,0:T(8,128)(2,1)S(1)}, bf16[128,1024]{1,0:T(8,128)(2,1)S(1)}, u32[]{:S(2)}, u32[]{:S(2)}) collective-permute-start(bf16[128,1024]{1,0:T(8,128)(2,1)S(1)} %add_convert_fusion.3), channel_id=1, source_target_pairs={{1,0},{2,1},{3,2},{4,3},{5,4},{6,5},{7,6},{9,8},{10,9},{11,10},{12... | collective-permute-start | bytes 786440 | tf_op jit(solution)/shard_map/while/body/eval_jaxpr/ppermute | solution.py:12
  457.1 10.4 %collective-permute-start.1 = (bf16[128,1024]{1,0:T(8,128)(2,1)S(1)}, bf16[128,1024]{1,0:T(8,128)(2,1)S(1)}, u32[]{:S(2)}, u32[]{:S(2)}) collective-permute-start(bf16[128,1024]{1,0:T(8,128)(2,1)S(1)} %add_convert_fusion.3), channel_id=1, source_target_pairs={{1,0},{2,1},{3,2},{4,3},{5,4},{6,5},{7,6},{9,8},{10,9},{11,10},{12... | collective-permute-start | bytes 786440 | tf_op jit(solution)/shard_map/while/body/eval_jaxpr/ppermute | solution.py:12
  473.0 3.5 copy-start.3
  482.1 190.3 %reduce-scatter.8.cloned.1.call-start = ((), (), s32[]{:S(2)}) async-start(), calls=%async_computation.4 | async-start | bytes 1179648 | tf_op jit(solution)/shard_map/reduce_scatter | solution.py:113
  489.4 256.8 %reduce-scatter.12.cloned.1.call-start = ((), (), s32[]{:S(2)}) async-start(), calls=%async_computation.6 | async-start | bytes 2228224 | tf_op jit(solution)/shard_map/reduce_scatter | solution.py:128
  492.3 3.3 copy-start.8
  499.0 135.0 %copy-start.6 = (u32[128]{0:T(128)S(1)}, u32[128]{0:T(128)}, u32[]{:S(2)}) copy-start(u32[128]{0:T(128)} %constant.72) | copy-start | bytes 1540
  499.0 247.2 %copy-start.1 = (bf16[1,1024,1024]{2,1,0:T(8,128)(2,1)S(1)}, bf16[1,1024,1024]{2,1,0:T(8,128)(2,1)}, u32[]{:S(2)}) copy-start(bf16[1,1024,1024]{2,1,0:T(8,128)(2,1)} %param.14) | copy-start | bytes 6291460
  617.3 18.0 %collective-permute-start.3 = (bf16[1024,60]{0,1:T(8,128)(2,1)S(1)}, bf16[1024,60]{0,1:T(8,128)(2,1)S(1)}, u32[]{:S(2)}, u32[]{:S(2)}) collective-permute-start(bf16[1024,60]{0,1:T(8,128)(2,1)S(1)} %slice.3), channel_id=1, source_target_pairs={{0,8},{8,16},{16,24},{24,32},{32,40},{40,48},{48,56},{56,64},{64,7... | collective-permute-start | bytes 368648
  627.5 8.2 %collective-permute-start.2 = (bf16[1024,60]{0,1:T(8,128)(2,1)S(1)}, bf16[1024,60]{0,1:T(8,128)(2,1)}, u32[]{:S(2)}, u32[]{:S(2)}) collective-permute-start(bf16[1024,60]{0,1:T(8,128)(2,1)S(1)} %slice.2), channel_id=1, source_target_pairs={{0,8},{8,16},{16,24},{24,32},{32,40},{40,48},{48,56},{56,64},{64,7... | collective-permute-start | bytes 368648
Sparse Core Ops, SparseCore 0:
  10.4 113.4 all-gather.6
  126.3 77.2 all-gather.4
  482.2 148.7 reduce-scatter.9
  633.8 38.5 reduce-scatter.7
  676.8 69.3 reduce-scatter.11
